TPU v7x, 32 devices: a whole 2x2x4 slice. The times are simulated.
32 devices in a mesh: ctx: 8 (over z, x), chan: 2 (over core), dp: 2 (over y).
Axes of the slice: x: 2, y: 2, z: 4, core: 2. Of those that a mesh axis runs over, the one named last changes fastest.
Arguments:
- q_stream: bfloat16 [2, 2048, 4096], P('dp', 'ctx', 'chan'), may hold values from -6 to 6
- k_stream: bfloat16 [2, 2048, 4096], P('dp', 'ctx', 'chan'), may hold values from -6 to 6
- v_stream: bfloat16 [2, 2048, 4096], P('dp', 'ctx', 'chan'), may hold values from -6 to 6
- out_grad: bfloat16 [2, 2048, 4096], P('dp', 'ctx', 'chan'), may hold values from -6 to 6
- norm_gain: float32 [4096], P('chan'), may hold values from 0.1 to 1.9
- residue: float32 [4096, 16], P('chan'), may hold values from -6 to 6
- rate: float32 [4096, 16], P('chan'), may hold values from -1.5 to 6
Outputs:
- y_out: bfloat16 [2, 2048, 4096], P('dp', 'ctx', 'chan')
- grad_q: bfloat16 [2, 2048, 4096], P('dp', 'ctx', 'chan')
- grad_k: bfloat16 [2, 2048, 4096], P('dp', 'ctx', 'chan')
- grad_v: bfloat16 [2, 2048, 4096], P('dp', 'ctx', 'chan')
- grad_residue: float32 [4096, 16], P('chan')
- grad_rate: float32 [4096, 16], P('chan')
- grad_gain: float32 [4096], P('chan')
All inputs are finite; a program needn't handle non-finite values.
Results may differ from a plain program's by a relative error of at most 0.0051.
Values may be sent and summed in bfloat16 or wider, within the bound.
No kernel may reach another device: no remote copies, remote signals or barrier semaphores. Data moves between devices by JAX's collectives and lax.ppermute only.
A program may use at most 128 MiB of HBM per device.

v0:
```python
import math
import jax
import jax.numpy as jnp
from jax import lax
from jax.sharding import PartitionSpec as P

D = 4096
highest = lax.Precision.HIGHEST
epsilon = 1e-06


def modal(decays, angles, parity, seq_len, with_slope):
    shrink = jnp.exp(-decays)[None, :]
    gap_one = (-jnp.expm1(-decays))[None, :]
    tail_val = jnp.exp(-decays * seq_len)[None, :]
    gap_all = (-jnp.expm1(-decays * seq_len))[None, :]
    odd_rows = (parity > 0)[:, None]
    numer = jnp.where(odd_rows, 1.0 + tail_val, gap_all)
    half_sin = jnp.sin(angles * 0.5)[:, None]
    full_sin = jnp.sin(angles)[:, None]
    den_real = gap_one + 2.0 * shrink * half_sin * half_sin
    den_imag = shrink * full_sin
    magnitude = den_real * den_real + den_imag * den_imag
    value_real = numer * den_real / magnitude
    value_imag = -numer * den_imag / magnitude
    if not with_slope:
        return (value_real, value_imag)
    power = jnp.where(odd_rows, -tail_val, tail_val)
    z_real = shrink * jnp.cos(angles)[:, None]
    z_imag = -shrink * full_sin
    top_real = seq_len * power * den_real - numer * z_real
    top_imag = seq_len * power * den_imag - numer * z_imag
    square_real = den_real * den_real - den_imag * den_imag
    square_imag = 2.0 * den_real * den_imag
    quartic = magnitude * magnitude
    slope_real = (top_real * square_real + top_imag * square_imag) / quartic
    slope_imag = (top_imag * square_real - top_real * square_imag) / quartic
    return (value_real, value_imag, slope_real, slope_imag)


def gating(conv, q_part, grad_part, norm_gain):
    q_float = q_part.astype(jnp.float32)
    grad_float = grad_part.astype(jnp.float32)
    mixed = q_float * conv
    scaled = norm_gain * grad_float
    squares, inner_sum = lax.psum(
        (jnp.sum(mixed * mixed, axis=-1), jnp.sum(scaled * mixed, axis=-1)), "chan"
    )
    inv_rms = lax.rsqrt(squares / D + epsilon)[..., None]
    inner_sum = inner_sum[..., None]
    y_part = (norm_gain * mixed * inv_rms).astype(jnp.bfloat16)
    mixed_grad = inv_rms * scaled - mixed * (inv_rms * inv_rms * inv_rms * inner_sum / D)
    grad_q = (mixed_grad * conv).astype(jnp.bfloat16)
    gate_grad = mixed_grad * q_float
    gain_part = jnp.sum((grad_float * mixed * inv_rms).reshape(-1, conv.shape[-1]), axis=0)
    return (y_part, grad_q, gate_grad, gain_part)


def transform_plan(q_stream, k_stream, v_stream, out_grad, norm_gain, residue, rate):
    ctx_count = lax.axis_size("ctx")
    ctx_rank = lax.axis_index("ctx")
    batch_rows, length, channels = q_stream.shape
    slice_len = length // ctx_count
    seq_len = length * ctx_count
    period = 2 * seq_len
    is_first = ctx_rank == 0
    slots = jnp.arange(ctx_count, dtype=jnp.int32)
    slot_angle = (slots[:, None] * slots[None, :] % (2 * ctx_count)).astype(jnp.float32) * (
        math.pi / ctx_count
    )
    signs = (1 - 2 * (slots % 2)).astype(jnp.float32)
    lead_row = slots[:, None] == 0
    lead_col = slots[None, :] == 0
    forward_real = jnp.where(lead_row, 1.0, jnp.cos(slot_angle))
    forward_imag = jnp.where(lead_row, signs[None, :], -jnp.sin(slot_angle))
    inverse_real = jnp.where(lead_col, 1.0, 2.0 * jnp.cos(slot_angle)) / period
    inverse_imag = jnp.where(lead_col, signs[:, None], -2.0 * jnp.sin(slot_angle)) / period
    columns = jnp.arange(length, dtype=jnp.int32)
    freq_a = jnp.where(is_first, 0, ctx_rank) + 2 * ctx_count * columns
    freq_b = jnp.where(is_first, ctx_count, ctx_rank) + 2 * ctx_count * columns

    def twiddle(freq):
        phase = (freq[:, None] * columns[None, :] % period).astype(jnp.float32) * (
            2.0 * math.pi / period
        )
        return (jnp.cos(phase), jnp.sin(phase))

    cosine_a, sine_a = twiddle(freq_a)
    cosine_b, sine_b = twiddle(freq_b)
    angles_a = freq_a.astype(jnp.float32) * (2.0 * math.pi / period)
    angles_b = freq_b.astype(jnp.float32) * (2.0 * math.pi / period)
    parity_a = freq_a % 2
    parity_b = freq_b % 2

    def spectrum(slices):
        slot_real = jnp.einsum("kb,xbjc->xkjc", forward_real, slices, precision=highest)
        slot_imag = jnp.einsum("kb,xbjc->xkjc", forward_imag, slices, precision=highest)
        rows_real, rows_imag = (
            lax.all_to_all(slot_real, "ctx", split_axis=1, concat_axis=1, tiled=True),
            lax.all_to_all(slot_imag, "ctx", split_axis=1, concat_axis=1, tiled=True),
        )
        rows_real = rows_real.reshape(batch_rows, length, channels)
        rows_imag = rows_imag.reshape(batch_rows, length, channels)
        a_real = jnp.einsum("kj,xjc->xkc", cosine_a, rows_real, precision=highest)
        a_imag = -jnp.einsum("kj,xjc->xkc", sine_a, rows_real, precision=highest)
        b_real = jnp.einsum("kj,xjc->xkc", cosine_b, rows_imag, precision=highest)
        b_imag = -jnp.einsum("kj,xjc->xkc", sine_b, rows_imag, precision=highest)
        return (a_real, a_imag, b_real, b_imag)

    def positions(spec):
        g_ar, g_ai, g_br, g_bi = spec
        u_first = g_ar - g_bi
        u_second = g_ai + g_br
        x_first = jnp.where(is_first, g_ar, u_first)
        x_second = jnp.where(is_first, g_ai, u_second)
        y_first = jnp.where(is_first, g_br, u_second)
        y_second = jnp.where(is_first, -g_bi, u_first)
        out_real = jnp.einsum("kj,xkc->xjc", cosine_a, x_first, precision=highest) - jnp.einsum(
            "kj,xkc->xjc", sine_a, x_second, precision=highest
        )
        out_imag = jnp.einsum("kj,xkc->xjc", cosine_b, y_first, precision=highest) + jnp.einsum(
            "kj,xkc->xjc", sine_b, y_second, precision=highest
        )
        out_real = out_real.reshape(batch_rows, ctx_count, slice_len, channels)
        out_imag = out_imag.reshape(batch_rows, ctx_count, slice_len, channels)
        recv_real, recv_imag = (
            lax.all_to_all(out_real, "ctx", split_axis=1, concat_axis=1, tiled=True),
            lax.all_to_all(out_imag, "ctx", split_axis=1, concat_axis=1, tiled=True),
        )
        return jnp.einsum("bk,xkjc->xbjc", inverse_real, recv_real, precision=highest) + jnp.einsum(
            "bk,xkjc->xbjc", inverse_imag, recv_imag, precision=highest
        )

    def multiply(spec, kernel_rows, flip):
        s_ar, s_ai, s_br, s_bi = spec
        h_ar, h_ai, h_br, h_bi = kernel_rows
        if flip:
            h_ai = -h_ai
            h_bi = -h_bi
        return (
            s_ar * h_ar - s_ai * h_ai,
            s_ai * h_ar + s_ar * h_ai,
            s_br * h_br - s_bi * h_bi,
            s_bi * h_br + s_br * h_bi,
        )

    decays = jnp.exp(rate) / seq_len
    flat_decays = decays.reshape(-1)
    mode_count = residue.shape[1]
    block = math.gcd(length, 64)
    block_count = length // block
    block_ids = jnp.arange(block_count, dtype=jnp.int32)

    def kernel_block(carry, block_index):
        row_start = block_index * block
        pieces_now = []
        for angles, parity in ((angles_a, parity_a), (angles_b, parity_b)):
            angle_rows = lax.dynamic_slice_in_dim(angles, row_start, block)
            parity_rows = lax.dynamic_slice_in_dim(parity, row_start, block)
            f_real, f_imag = modal(flat_decays, angle_rows, parity_rows, seq_len, False)
            pieces_now.append(
                jnp.sum(f_real.reshape(block, channels, mode_count) * residue, axis=-1)
            )
            pieces_now.append(
                jnp.sum(f_imag.reshape(block, channels, mode_count) * residue, axis=-1)
            )
        return (carry, tuple(pieces_now))

    _, kernel_pieces = lax.scan(kernel_block, 0.0, block_ids)
    kernel_rows = tuple((piece.reshape(length, channels) for piece in kernel_pieces))
    value_blocks = (k_stream.astype(jnp.float32) * v_stream.astype(jnp.float32)).astype(
        jnp.bfloat16
    )
    value_sl = lax.all_to_all(
        value_blocks.reshape(batch_rows, ctx_count, slice_len, channels),
        "ctx",
        split_axis=1,
        concat_axis=1,
        tiled=True,
    ).astype(jnp.float32)
    value_spec = spectrum(value_sl)
    conv_sl = positions(multiply(value_spec, kernel_rows, False))
    conv_blk = lax.all_to_all(conv_sl, "ctx", split_axis=1, concat_axis=1, tiled=True).reshape(
        batch_rows, length, channels
    )
    y_out, grad_q, gate_blk, gain_part = gating(conv_blk, q_stream, out_grad, norm_gain)
    gate_sl = lax.all_to_all(
        gate_blk.reshape(batch_rows, ctx_count, slice_len, channels),
        "ctx",
        split_axis=1,
        concat_axis=1,
        tiled=True,
    )
    gate_spec = spectrum(gate_sl)
    grad_sl = positions(multiply(gate_spec, kernel_rows, True))
    value_grad = lax.all_to_all(grad_sl, "ctx", split_axis=1, concat_axis=1, tiled=True).reshape(
        batch_rows, length, channels
    )
    grad_k = (value_grad * v_stream.astype(jnp.float32)).astype(jnp.bfloat16)
    grad_v = (value_grad * k_stream.astype(jnp.float32)).astype(jnp.bfloat16)

    def true_rows(spec):
        s_ar, s_ai, s_br, s_bi = spec
        return (
            jnp.where(is_first, s_ar, s_ar - s_bi),
            jnp.where(is_first, s_ai, s_ai + s_br),
            s_br,
            s_bi,
        )

    z_ar, z_ai, z_br, z_bi = true_rows(value_spec)
    g_ar, g_ai, g_br, g_bi = true_rows(gate_spec)
    cross_ar = jnp.sum(g_ar * z_ar + g_ai * z_ai, axis=0)
    cross_ai = jnp.sum(g_ai * z_ar - g_ar * z_ai, axis=0)
    cross_br = jnp.sum(g_br * z_br + g_bi * z_bi, axis=0)
    cross_bi = jnp.sum(g_bi * z_br - g_br * z_bi, axis=0)
    weight_a = jnp.where(is_first, 1.0, 2.0) / period
    weight_b = jnp.where(is_first, 1.0, 0.0) / period

    def grad_block(totals, block_index):
        row_start = block_index * block
        sums_now = []
        for angles, parity, cross_real, cross_imag in (
            (angles_a, parity_a, cross_ar, cross_ai),
            (angles_b, parity_b, cross_br, cross_bi),
        ):
            angle_rows = lax.dynamic_slice_in_dim(angles, row_start, block)
            parity_rows = lax.dynamic_slice_in_dim(parity, row_start, block)
            real_rows = lax.dynamic_slice_in_dim(cross_real, row_start, block)[:, :, None]
            imag_rows = lax.dynamic_slice_in_dim(cross_imag, row_start, block)[:, :, None]
            f_real, f_imag, d_real, d_imag = modal(
                flat_decays, angle_rows, parity_rows, seq_len, True
            )
            shape_three = (block, channels, mode_count)
            sums_now.append(
                jnp.sum(
                    real_rows * f_real.reshape(shape_three)
                    + imag_rows * f_imag.reshape(shape_three),
                    axis=0,
                )
            )
            sums_now.append(
                jnp.sum(
                    real_rows * d_real.reshape(shape_three)
                    + imag_rows * d_imag.reshape(shape_three),
                    axis=0,
                )
            )
        return (tuple((total + part for total, part in zip(totals, sums_now))), None)

    zero_modes = jnp.zeros((channels, mode_count), jnp.float32)
    (res_a, slope_a, res_b, slope_b), _ = lax.scan(
        grad_block, (zero_modes, zero_modes, zero_modes, zero_modes), block_ids
    )
    res_part = weight_a * res_a + weight_b * res_b
    rate_part = decays * residue * (weight_a * slope_a + weight_b * slope_b)
    return (y_out, grad_q, grad_k, grad_v, res_part, rate_part, gain_part)


def shards(q_stream, k_stream, v_stream, out_grad, norm_gain, residue, rate):
    results = transform_plan(q_stream, k_stream, v_stream, out_grad, norm_gain, residue, rate)
    y_out, grad_q, grad_k, grad_v, res_part, rate_part, gain_part = results
    grad_residue, grad_rate, grad_gain = lax.psum((res_part, rate_part, gain_part), ("ctx", "dp"))
    return (y_out, grad_q, grad_k, grad_v, grad_residue, grad_rate, grad_gain)


def solution(mesh):
    in_specs = (
        P("dp", "ctx", "chan"),
        P("dp", "ctx", "chan"),
        P("dp", "ctx", "chan"),
        P("dp", "ctx", "chan"),
        P("chan"),
        P("chan", None),
        P("chan", None),
    )
    out_specs = (
        P("dp", "ctx", "chan"),
        P("dp", "ctx", "chan"),
        P("dp", "ctx", "chan"),
        P("dp", "ctx", "chan"),
        P("chan", None),
        P("chan", None),
        P("chan"),
    )
    return jax.shard_map(shards, mesh=mesh, in_specs=in_specs, out_specs=out_specs, check_vma=False)
```

profile of v0, /device:TPU:0, one launch (start us, length us, event | category | flops | bytes accessed | tf_op | source)
XLA Modules:
  0.0 1118.8 jit_solution(14108941958894904162)
XLA Ops:
  10.1 7.3 all-to-all-start
  18.8 24.3 %all-to-all-done = bf16[1,8,32,2048]{3,2,0,1:T(8,128)(2,1)S(1)} async-done(((bf16[1,8,32,2048]{3,2,0,1:T(8,128)(2,1)}), bf16[1,8,32,2048]{3,2,0,1:T(8,128)(2,1)S(1)}, u32[]{:S(2)}, u32[]{:S(2)}) %all-to-all-start) | async-done | bytes 1048608 | tf_op jit(solution)/shard_map/all_to_all | solution.py:174
  57.4 41.7 %all-to-all-done.2 = f32[1,8,32,2048]{3,2,0,1:T(8,128)S(1)} async-done(((f32[1,8,32,2048]{3,2,0,1:T(8,128)}), f32[1,8,32,2048]{3,2,0,1:T(8,128)S(1)}, u32[]{:S(2)}, u32[]{:S(2)}) %all-to-all-start.2) | async-done | bytes 2097184 | tf_op jit(solution)/shard_map/all_to_all | solution.py:100
  99.1 4.6 all-to-all-start.1
  103.7 114.4 %while.39 = (s32[]{:T(128)}, f32[4,64,2048]{2,1,0:T(8,128)}, f32[4,64,2048]{2,1,0:T(8,128)}, f32[4,64,2048]{2,1,0:T(8,128)}, f32[4,64,2048]{2,1,0:T(8,128)}, /*i...) while((s32[]{:T(128)}, f32[4,64,2048]{2,1,0:T(8,128)}, ...), condition=%wide.region_5.6_spmd, body=%wide.region_0.5_spmd.sunk | while | flops 70910216 | bytes 10621447 | solution.py:169
  115.0 15.1 %fusion.311 = (f32[64,2048]{1,0:T(8,128)S(1)}, f32[64,2048]{1,0:T(8,128)S(1)}, f32[64,2048]{1,0:T(8,128)S(1)}, f32[64,2048]{1,0:T(8,128)S(1)}) fusion(f32[64]{0:T(128)S(1)} %get-tuple-element.922, f32[64]{0:T(128)S(1)} %get-tuple-element.923, f32[2048,16]{0,1:T(8,128)S(1)} %get-tuple-element.1021, f32[2048,16]{0,1:T(8,128)S(1)} %copy.198, ...), kind=kLoop, calls=%fused_computation.19.clone.1 | loop fusion | flops 70778880 | bytes 2884736 | tf_op jit(solution)/shard_map/while/body/eval_jaxpr/reduce_sum | solution.py:165
  143.7 15.1 %fusion.311 = (f32[64,2048]{1,0:T(8,128)S(1)}, f32[64,2048]{1,0:T(8,128)S(1)}, f32[64,2048]{1,0:T(8,128)S(1)}, f32[64,2048]{1,0:T(8,128)S(1)}) fusion(f32[64]{0:T(128)S(1)} %get-tuple-element.922, f32[64]{0:T(128)S(1)} %get-tuple-element.923, f32[2048,16]{0,1:T(8,128)S(1)} %get-tuple-element.1021, f32[2048,16]{0,1:T(8,128)S(1)} %copy.198, ...), kind=kLoop, calls=%fused_computation.19.clone.1 | loop fusion | flops 70778880 | bytes 2884736 | tf_op jit(solution)/shard_map/while/body/eval_jaxpr/reduce_sum | solution.py:165
  172.2 15.1 %fusion.311 = (f32[64,2048]{1,0:T(8,128)S(1)}, f32[64,2048]{1,0:T(8,128)S(1)}, f32[64,2048]{1,0:T(8,128)S(1)}, f32[64,2048]{1,0:T(8,128)S(1)}) fusion(f32[64]{0:T(128)S(1)} %get-tuple-element.922, f32[64]{0:T(128)S(1)} %get-tuple-element.923, f32[2048,16]{0,1:T(8,128)S(1)} %get-tuple-element.1021, f32[2048,16]{0,1:T(8,128)S(1)} %copy.198, ...), kind=kLoop, calls=%fused_computation.19.clone.1 | loop fusion | flops 70778880 | bytes 2884736 | tf_op jit(solution)/shard_map/while/body/eval_jaxpr/reduce_sum | solution.py:165
  200.8 15.1 %fusion.311 = (f32[64,2048]{1,0:T(8,128)S(1)}, f32[64,2048]{1,0:T(8,128)S(1)}, f32[64,2048]{1,0:T(8,128)S(1)}, f32[64,2048]{1,0:T(8,128)S(1)}) fusion(f32[64]{0:T(128)S(1)} %get-tuple-element.922, f32[64]{0:T(128)S(1)} %get-tuple-element.923, f32[2048,16]{0,1:T(8,128)S(1)} %get-tuple-element.1021, f32[2048,16]{0,1:T(8,128)S(1)} %copy.198, ...), kind=kLoop, calls=%fused_computation.19.clone.1 | loop fusion | flops 70778880 | bytes 2884736 | tf_op jit(solution)/shard_map/while/body/eval_jaxpr/reduce_sum | solution.py:165
  229.2 5.9 convolution_bitcast_fusion.7
  235.2 6.7 fusion.38
  241.9 8.5 multiply_subtract_fusion.2
  250.4 9.0 multiply_add_fusion.6
  262.7 4.8 convolution_subtract_fusion.1
  267.5 6.1 all-to-all-start.3
  273.6 4.9 fusion.51
  278.6 4.7 convolution_add_fusion.3
  283.2 37.7 %all-to-all-done.3 = f32[1,8,32,2048]{3,2,0,1:T(8,128)} async-done(((f32[1,8,32,2048]{3,2,0,1:T(8,128)}), f32[1,8,32,2048]{3,2,0,1:T(8,128)}, u32[]{:S(2)}, u32[]{:S(2)}) %all-to-all-start.3) | async-done | bytes 2097184 | tf_op jit(solution)/shard_map/all_to_all | solution.py:127
  325.0 6.2 fusion.68
  331.2 42.2 %all-to-all-done.4 = f32[1,8,32,2048]{3,2,0,1:T(8,128)S(1)} async-done(((f32[1,8,32,2048]{3,2,0,1:T(8,128)}), f32[1,8,32,2048]{3,2,0,1:T(8,128)S(1)}, u32[]{:S(2)}, u32[]{:S(2)}) %all-to-all-start.4) | async-done | bytes 2097184 | tf_op jit(solution)/shard_map/all_to_all | solution.py:128
  373.3 4.9 fusion.37
  379.5 51.9 %all_to_all.60 = f32[1,8,32,2048]{3,2,0,1:T(8,128)S(1)} all-to-all(f32[1,8,32,2048]{3,2,0,1:T(8,128)S(1)} %copy.131), channel_id=1, replica_groups=mesh['ctx'=8,'chan'=2,'dp'=2] {'ctx'}, dimensions={1} | all-to-all | bytes 4194304 | tf_op jit(solution)/shard_map/all_to_all | solution.py:183
  442.2 52.1 %all_to_all.61 = f32[1,8,32,2048]{3,2,0,1:T(8,128)S(1)} all-to-all(f32[1,8,32,2048]{3,2,0,1:T(8,128)S(1)} %bitcast.214), channel_id=1, replica_groups=mesh['ctx'=8,'chan'=2,'dp'=2] {'ctx'}, dimensions={1} | all-to-all | bytes 4194304 | tf_op jit(solution)/shard_map/all_to_all | solution.py:187
  510.3 41.6 %all-to-all-done.8 = f32[1,8,32,2048]{3,2,0,1:T(8,128)} async-done(((f32[1,8,32,2048]{3,2,0,1:T(8,128)}), f32[1,8,32,2048]{3,2,0,1:T(8,128)}, u32[]{:S(2)}, u32[]{:S(2)}) %all-to-all-start.8) | async-done | bytes 2097184 | tf_op jit(solution)/shard_map/all_to_all | solution.py:100
  555.7 7.2 convolution_bitcast_fusion
  562.9 7.3 convolution_bitcast_fusion.1
  570.2 33.8 %all-to-all-done.7 = f32[1,8,32,2048]{3,2,0,1:T(8,128)S(1)} async-done(((f32[1,8,32,2048]{3,2,0,1:T(8,128)}), f32[1,8,32,2048]{3,2,0,1:T(8,128)S(1)}, u32[]{:S(2)}, u32[]{:S(2)}) %all-to-all-start.7) | async-done | bytes 2097184 | tf_op jit(solution)/shard_map/all_to_all | solution.py:99
  603.9 5.9 convolution_bitcast_fusion.3
  609.8 18.4 %subtract_bitcast_fusion.1 = (f32[256,2048]{0,1:T(8,128)}, f32[256,2048]{0,1:T(8,128)}, f32[256,2048]{0,1:T(8,128)}, f32[256,2048]{0,1:T(8,128)}, f32[1,256,2048...) fusion(f32[1,256,2048]{1,2,0:T(8,128)} %copy-done.9, ...), kind=kOutput, calls=%fused_computation.170 | convolution fusion | flops 1630928896 | bytes 41944064 | tf_op jit(solution)/shard_map/kj,xjc->xkc/dot_general | solution.py:104
  631.5 4.6 convolution_subtract_fusion
  636.0 4.5 all-to-all-start.9
  640.6 5.6 fusion.56
  646.1 4.7 convolution_add_fusion.1
  650.8 37.5 %all-to-all-done.9 = f32[1,8,32,2048]{3,2,0,1:T(8,128)} async-done(((f32[1,8,32,2048]{3,2,0,1:T(8,128)}), f32[1,8,32,2048]{3,2,0,1:T(8,128)}, u32[]{:S(2)}, u32[]{:S(2)}) %all-to-all-start.9) | async-done | bytes 2097184 | tf_op jit(solution)/shard_map/all_to_all | solution.py:127
  692.8 69.5 %psum.39 = f32[2048]{0:T(1024)} all-reduce(f32[2048]{0:T(1024)S(1)} %get-tuple-element.596), channel_id=1, replica_groups=mesh['ctx'=8,'chan'=2,'dp'=2] {'ctx','dp'}, use_global_device_ids=true, to_apply=%region_19.20 | all-reduce | flops 2048 | bytes 16384 | tf_op jit(solution)/shard_map/psum | solution.py:263
  772.1 6.2 fusion.60
  778.3 5.5 fusion.36
  786.3 7.2 all-to-all-start.11
  794.2 203.1 %while.40 = (s32[]{:T(128)}, f32[2048,16]{0,1:T(8,128)}, f32[2048,16]{0,1:T(8,128)}, f32[2048,16]{0,1:T(8,128)}, f32[2048,16]{0,1:T(8,128)}, /*index=5*/s32[4]{0...) while((s32[]{:T(128)}, f32[2048,16]{0,1:T(8,128)}, ...), condition=%wide.region_15.16_spmd.clone, body=%wide.region_10.15_spmd.clone.sunk | while | flops 180650240 | bytes 40907724 | solution.py:252
  812.7 13.5 %add_reduce_fusion.8 = (f32[2048,16]{0,1:T(8,128)S(1)}, f32[2048,16]{0,1:T(8,128)S(1)}) fusion(f32[64]{0:T(128)S(1)} %get-tuple-element.965, f32[64,2048]{1,0:T(8,128)S(1)} %copy-done, f32[64]{0:T(128)S(1)} %get-tuple-element.966, f32[64]{0:T(128)S(1)} %get-tuple-element.967, f32[64,2048]{1,0:T(8,128)S(1)} %copy-done.1, f32[2048,16]{0,1:T(8,128)S(1)} %copy.203, ...), kind=kLoop, calls=%fused_computation.71.clone.1 | loop fusion | flops 90112000 | bytes 2360128 | tf_op jit(solution)/shard_map/while/body/eval_jaxpr/reduce_sum | solution.py:243
  830.1 12.9 %add_reduce_fusion.7 = (f32[2048,16]{0,1:T(8,128)S(1)}, f32[2048,16]{0,1:T(8,128)S(1)}) fusion(f32[2048,16]{0,1:T(8,128)S(1)} %copy.203, f32[64]{0:T(128)S(1)} %get-tuple-element.954, f32[2048,16]{0,1:T(8,128)S(1)} %copy.204, f32[2048,16]{0,1:T(8,128)S(1)} %copy.205, f32[64,2048]{1,0:T(8,128)S(1)} %constant_dynamic-slice_fusion.8, ...), kind=kLoop, calls=%fused_computation.75.clone.1 | loop fusion | flops 90112000 | bytes 2360128 | tf_op jit(solution)/shard_map/while/body/eval_jaxpr/reduce_sum | solution.py:243
  862.8 13.5 %add_reduce_fusion.8 = (f32[2048,16]{0,1:T(8,128)S(1)}, f32[2048,16]{0,1:T(8,128)S(1)}) fusion(f32[64]{0:T(128)S(1)} %get-tuple-element.965, f32[64,2048]{1,0:T(8,128)S(1)} %copy-done, f32[64]{0:T(128)S(1)} %get-tuple-element.966, f32[64]{0:T(128)S(1)} %get-tuple-element.967, f32[64,2048]{1,0:T(8,128)S(1)} %copy-done.1, f32[2048,16]{0,1:T(8,128)S(1)} %copy.203, ...), kind=kLoop, calls=%fused_computation.71.clone.1 | loop fusion | flops 90112000 | bytes 2360128 | tf_op jit(solution)/shard_map/while/body/eval_jaxpr/reduce_sum | solution.py:243
  881.1 12.9 %add_reduce_fusion.7 = (f32[2048,16]{0,1:T(8,128)S(1)}, f32[2048,16]{0,1:T(8,128)S(1)}) fusion(f32[2048,16]{0,1:T(8,128)S(1)} %copy.203, f32[64]{0:T(128)S(1)} %get-tuple-element.954, f32[2048,16]{0,1:T(8,128)S(1)} %copy.204, f32[2048,16]{0,1:T(8,128)S(1)} %copy.205, f32[64,2048]{1,0:T(8,128)S(1)} %constant_dynamic-slice_fusion.8, ...), kind=kLoop, calls=%fused_computation.75.clone.1 | loop fusion | flops 90112000 | bytes 2360128 | tf_op jit(solution)/shard_map/while/body/eval_jaxpr/reduce_sum | solution.py:243
  913.7 13.5 %add_reduce_fusion.8 = (f32[2048,16]{0,1:T(8,128)S(1)}, f32[2048,16]{0,1:T(8,128)S(1)}) fusion(f32[64]{0:T(128)S(1)} %get-tuple-element.965, f32[64,2048]{1,0:T(8,128)S(1)} %copy-done, f32[64]{0:T(128)S(1)} %get-tuple-element.966, f32[64]{0:T(128)S(1)} %get-tuple-element.967, f32[64,2048]{1,0:T(8,128)S(1)} %copy-done.1, f32[2048,16]{0,1:T(8,128)S(1)} %copy.203, ...), kind=kLoop, calls=%fused_computation.71.clone.1 | loop fusion | flops 90112000 | bytes 2360128 | tf_op jit(solution)/shard_map/while/body/eval_jaxpr/reduce_sum | solution.py:243
  932.0 12.9 %add_reduce_fusion.7 = (f32[2048,16]{0,1:T(8,128)S(1)}, f32[2048,16]{0,1:T(8,128)S(1)}) fusion(f32[2048,16]{0,1:T(8,128)S(1)} %copy.203, f32[64]{0:T(128)S(1)} %get-tuple-element.954, f32[2048,16]{0,1:T(8,128)S(1)} %copy.204, f32[2048,16]{0,1:T(8,128)S(1)} %copy.205, f32[64,2048]{1,0:T(8,128)S(1)} %constant_dynamic-slice_fusion.8, ...), kind=kLoop, calls=%fused_computation.75.clone.1 | loop fusion | flops 90112000 | bytes 2360128 | tf_op jit(solution)/shard_map/while/body/eval_jaxpr/reduce_sum | solution.py:243
  964.6 13.5 %add_reduce_fusion.8 = (f32[2048,16]{0,1:T(8,128)S(1)}, f32[2048,16]{0,1:T(8,128)S(1)}) fusion(f32[64]{0:T(128)S(1)} %get-tuple-element.965, f32[64,2048]{1,0:T(8,128)S(1)} %copy-done, f32[64]{0:T(128)S(1)} %get-tuple-element.966, f32[64]{0:T(128)S(1)} %get-tuple-element.967, f32[64,2048]{1,0:T(8,128)S(1)} %copy-done.1, f32[2048,16]{0,1:T(8,128)S(1)} %copy.203, ...), kind=kLoop, calls=%fused_computation.71.clone.1 | loop fusion | flops 90112000 | bytes 2360128 | tf_op jit(solution)/shard_map/while/body/eval_jaxpr/reduce_sum | solution.py:243
  982.9 12.9 %add_reduce_fusion.7 = (f32[2048,16]{0,1:T(8,128)S(1)}, f32[2048,16]{0,1:T(8,128)S(1)}) fusion(f32[2048,16]{0,1:T(8,128)S(1)} %copy.203, f32[64]{0:T(128)S(1)} %get-tuple-element.954, f32[2048,16]{0,1:T(8,128)S(1)} %copy.204, f32[2048,16]{0,1:T(8,128)S(1)} %copy.205, f32[64,2048]{1,0:T(8,128)S(1)} %constant_dynamic-slice_fusion.8, ...), kind=kLoop, calls=%fused_computation.75.clone.1 | loop fusion | flops 90112000 | bytes 2360128 | tf_op jit(solution)/shard_map/while/body/eval_jaxpr/reduce_sum | solution.py:243
  1004.8 103.6 %all-reduce.3.cloned.1.call-done = (f32[2048,16]{0,1:T(8,128)}, f32[2048,16]{0,1:T(8,128)}) async-done(((f32[2048,16]{0,1:T(8,128)}, f32[2048,16]{0,1:T(8,128)}), (f32[2048,16]{0,1:T(8,128)}, f32[2048,16]{0,1:T(8,128)})) %all-reduce.3.cloned.1.call-update) | async-done | bytes 262160 | tf_op jit(solution)/shard_map/psum | solution.py:263
  (439 shorter events, 244.7 us)
Async XLA Ops:
  7.2 10.2 copy-start.36
  10.1 33.0 %all-to-all-start = ((bf16[1,8,32,2048]{3,2,0,1:T(8,128)(2,1)}), bf16[1,8,32,2048]{3,2,0,1:T(8,128)(2,1)S(1)}, u32[]{:S(2)}, u32[]{:S(2)}) async-start(bf16[1,8,32,2048]{3,2,0,1:T(8,128)(2,1)} %bitcast.6), calls=%async_computation | async-start | bytes 2097152 | tf_op jit(solution)/shard_map/all_to_all | solution.py:174
  47.1 52.0 %all-to-all-start.2 = ((f32[1,8,32,2048]{3,2,0,1:T(8,128)}), f32[1,8,32,2048]{3,2,0,1:T(8,128)S(1)}, u32[]{:S(2)}, u32[]{:S(2)}) async-start(f32[1,8,32,2048]{3,2,0,1:T(8,128)} %copy.120), calls=%async_computation.2 | async-start | bytes 4194304 | tf_op jit(solution)/shard_map/all_to_all | solution.py:100
  57.4 46.3 %copy-start.27 = (f32[2048,16]{0,1:T(8,128)S(1)}, f32[2048,16]{0,1:T(8,128)}, u32[]{:S(2)}) copy-start(f32[2048,16]{0,1:T(8,128)} %param.16) | copy-start | bytes 393220
  99.1 136.0 %all-to-all-start.1 = ((f32[1,8,32,2048]{3,2,0,1:T(8,128)}), f32[1,8,32,2048]{3,2,0,1:T(8,128)}, u32[]{:S(2)}, u32[]{:S(2)}) async-start(f32[1,8,32,2048]{3,2,0,1:T(8,128)} %copy.116), calls=%async_computation.1 | async-start | bytes 4194304 | tf_op jit(solution)/shard_map/all_to_all | solution.py:99
  235.1 6.7 copy-start.7
  235.1 6.7 copy-start.10
  235.2 6.7 copy-start.11
  241.9 8.5 copy-start.9
  241.9 8.5 copy-start.12
  241.9 8.5 copy-start.13
  250.4 9.0 copy-start.14
  250.4 12.2 %copy-start.16 = (f32[1,256,2048]{1,2,0:T(8,128)}, f32[1,256,2048]{1,2,0:T(8,128)S(1)}, u32[]{:S(2)}) copy-start(f32[1,256,2048]{1,2,0:T(8,128)S(1)} %get-tuple-element.692) | copy-start | bytes 6291460
  267.5 6.1 copy-start.17
  267.5 53.4 %all-to-all-start.3 = ((f32[1,8,32,2048]{3,2,0,1:T(8,128)}), f32[1,8,32,2048]{3,2,0,1:T(8,128)}, u32[]{:S(2)}, u32[]{:S(2)}) async-start(f32[1,8,32,2048]{3,2,0,1:T(8,128)} %bitcast.213), calls=%async_computation.3 | async-start | bytes 4194304 | tf_op jit(solution)/shard_map/all_to_all | solution.py:127
  320.9 52.4 %all-to-all-start.4 = ((f32[1,8,32,2048]{3,2,0,1:T(8,128)}), f32[1,8,32,2048]{3,2,0,1:T(8,128)S(1)}, u32[]{:S(2)}, u32[]{:S(2)}) async-start(f32[1,8,32,2048]{3,2,0,1:T(8,128)} %bitcast.44), calls=%async_computation.4 | async-start | bytes 4194304 | tf_op jit(solution)/shard_map/all_to_all | solution.py:128
  379.4 52.0 %copy-start.25 = (bf16[1,256,2048]{2,1,0:T(8,128)(2,1)S(1)}, bf16[1,256,2048]{2,1,0:T(8,128)(2,1)}, u32[]{:S(2)}) copy-start(bf16[1,256,2048]{2,1,0:T(8,128)(2,1)} %param.11) | copy-start | bytes 3145732
  500.1 51.8 %all-to-all-start.8 = ((f32[1,8,32,2048]{3,2,0,1:T(8,128)}), f32[1,8,32,2048]{3,2,0,1:T(8,128)}, u32[]{:S(2)}, u32[]{:S(2)}) async-start(f32[1,8,32,2048]{3,2,0,1:T(8,128)} %copy.137), calls=%async_computation.8 | async-start | bytes 4194304 | tf_op jit(solution)/shard_map/all_to_all | solution.py:100
  551.9 52.0 %all-to-all-start.7 = ((f32[1,8,32,2048]{3,2,0,1:T(8,128)}), f32[1,8,32,2048]{3,2,0,1:T(8,128)S(1)}, u32[]{:S(2)}, u32[]{:S(2)}) async-start(f32[1,8,32,2048]{3,2,0,1:T(8,128)} %copy.134), calls=%async_computation.7 | async-start | bytes 4194304 | tf_op jit(solution)/shard_map/all_to_all | solution.py:99
  628.2 7.8 copy-start.4
  628.2 7.8 copy-start.5
  636.0 52.3 %all-to-all-start.9 = ((f32[1,8,32,2048]{3,2,0,1:T(8,128)}), f32[1,8,32,2048]{3,2,0,1:T(8,128)}, u32[]{:S(2)}, u32[]{:S(2)}) async-start(f32[1,8,32,2048]{3,2,0,1:T(8,128)} %bitcast.212), calls=%async_computation.9 | async-start | bytes 4194304 | tf_op jit(solution)/shard_map/all_to_all | solution.py:127
  688.4 89.9 %all-to-all-start.10 = ((f32[1,8,32,2048]{3,2,0,1:T(8,128)}), f32[1,8,32,2048]{3,2,0,1:T(8,128)}, u32[]{:S(2)}, u32[]{:S(2)}) async-start(f32[1,8,32,2048]{3,2,0,1:T(8,128)} %bitcast.211), calls=%async_computation.10 | async-start | bytes 4194304 | tf_op jit(solution)/shard_map/all_to_all | solution.py:128
  786.3 214.4 %all-to-all-start.11 = ((f32[1,8,32,2048]{3,2,0,1:T(8,128)}), f32[1,8,32,2048]{3,2,0,1:T(8,128)}, u32[]{:S(2)}, u32[]{:S(2)}) async-start(f32[1,8,32,2048]{3,2,0,1:T(8,128)} %copy.148), calls=%async_computation.11 | async-start | bytes 4194304 | tf_op jit(solution)/shard_map/all_to_all | solution.py:196
  793.5 314.8 %all-reduce.3.cloned.1.call-start = ((), (), s32[]{:S(2)}) async-start(), calls=%async_computation.12 | async-start | bytes 524288 | tf_op jit(solution)/shard_map/psum | solution.py:263
  794.4 6.0 copy-start.23
  812.1 14.2 %copy-start.33 = (f32[2048,16]{0,1:T(8,128)S(1)}, f32[2048,16]{0,1:T(8,128)}, u32[]{:S(2)}) copy-start(f32[2048,16]{0,1:T(8,128)} %get-tuple-element.1055) | copy-start | bytes 393220 | tf_op jit(solution)/shard_map/while
  812.7 14.3 %copy-start.38 = (f32[256]{0:T(256)S(1)}, f32[256]{0:T(256)}, u32[]{:S(2)}) copy-start(f32[256]{0:T(256)} %get-tuple-element.1086) | copy-start | bytes 3076 | tf_op jit(solution)/shard_map/while
  827.7 15.4 %copy-start.29 = (f32[2048,16]{0,1:T(8,128)S(1)}, f32[2048,16]{0,1:T(8,128)}, u32[]{:S(2)}) copy-start(f32[2048,16]{0,1:T(8,128)} %get-tuple-element.1053) | copy-start | bytes 393220 | tf_op jit(solution)/shard_map/while
  827.7 15.4 %copy-start.31 = (f32[2048,16]{0,1:T(8,128)S(1)}, f32[2048,16]{0,1:T(8,128)}, u32[]{:S(2)}) copy-start(f32[2048,16]{0,1:T(8,128)} %get-tuple-element.1054) | copy-start | bytes 393220 | tf_op jit(solution)/shard_map/while
  828.8 15.7 %copy-start.24 = (f32[256,2048]{1,0:T(8,128)S(1)}, f32[256,2048]{1,0:T(8,128)}, u32[]{:S(2)}) copy-start(f32[256,2048]{1,0:T(8,128)} %copy-done.23) | copy-start | bytes 6291460 | tf_op jit(solution)/shard_map/while
  844.4 6.0 copy-start.23
  862.1 14.2 %copy-start.33 = (f32[2048,16]{0,1:T(8,128)S(1)}, f32[2048,16]{0,1:T(8,128)}, u32[]{:S(2)}) copy-start(f32[2048,16]{0,1:T(8,128)} %get-tuple-element.1055) | copy-start | bytes 393220 | tf_op jit(solution)/shard_map/while
  862.7 15.2 %copy-start.38 = (f32[256]{0:T(256)S(1)}, f32[256]{0:T(256)}, u32[]{:S(2)}) copy-start(f32[256]{0:T(256)} %get-tuple-element.1086) | copy-start | bytes 3076 | tf_op jit(solution)/shard_map/while
  878.6 15.4 %copy-start.29 = (f32[2048,16]{0,1:T(8,128)S(1)}, f32[2048,16]{0,1:T(8,128)}, u32[]{:S(2)}) copy-start(f32[2048,16]{0,1:T(8,128)} %get-tuple-element.1053) | copy-start | bytes 393220 | tf_op jit(solution)/shard_map/while
  878.6 15.4 %copy-start.31 = (f32[2048,16]{0,1:T(8,128)S(1)}, f32[2048,16]{0,1:T(8,128)}, u32[]{:S(2)}) copy-start(f32[2048,16]{0,1:T(8,128)} %get-tuple-element.1054) | copy-start | bytes 393220 | tf_op jit(solution)/shard_map/while
  879.7 15.7 %copy-start.24 = (f32[256,2048]{1,0:T(8,128)S(1)}, f32[256,2048]{1,0:T(8,128)}, u32[]{:S(2)}) copy-start(f32[256,2048]{1,0:T(8,128)} %copy-done.23) | copy-start | bytes 6291460 | tf_op jit(solution)/shard_map/while
  913.0 14.2 %copy-start.33 = (f32[2048,16]{0,1:T(8,128)S(1)}, f32[2048,16]{0,1:T(8,128)}, u32[]{:S(2)}) copy-start(f32[2048,16]{0,1:T(8,128)} %get-tuple-element.1055) | copy-start | bytes 393220 | tf_op jit(solution)/shard_map/while
  913.7 15.2 %copy-start.38 = (f32[256]{0:T(256)S(1)}, f32[256]{0:T(256)}, u32[]{:S(2)}) copy-start(f32[256]{0:T(256)} %get-tuple-element.1086) | copy-start | bytes 3076 | tf_op jit(solution)/shard_map/while
  929.5 15.4 %copy-start.29 = (f32[2048,16]{0,1:T(8,128)S(1)}, f32[2048,16]{0,1:T(8,128)}, u32[]{:S(2)}) copy-start(f32[2048,16]{0,1:T(8,128)} %get-tuple-element.1053) | copy-start | bytes 393220 | tf_op jit(solution)/shard_map/while
  929.5 15.4 %copy-start.31 = (f32[2048,16]{0,1:T(8,128)S(1)}, f32[2048,16]{0,1:T(8,128)}, u32[]{:S(2)}) copy-start(f32[2048,16]{0,1:T(8,128)} %get-tuple-element.1054) | copy-start | bytes 393220 | tf_op jit(solution)/shard_map/while
  930.6 15.7 %copy-start.24 = (f32[256,2048]{1,0:T(8,128)S(1)}, f32[256,2048]{1,0:T(8,128)}, u32[]{:S(2)}) copy-start(f32[256,2048]{1,0:T(8,128)} %copy-done.23) | copy-start | bytes 6291460 | tf_op jit(solution)/shard_map/while
  946.3 6.0 copy-start.23
  964.0 14.2 %copy-start.33 = (f32[2048,16]{0,1:T(8,128)S(1)}, f32[2048,16]{0,1:T(8,128)}, u32[]{:S(2)}) copy-start(f32[2048,16]{0,1:T(8,128)} %get-tuple-element.1055) | copy-start | bytes 393220 | tf_op jit(solution)/shard_map/while
  964.6 15.2 %copy-start.38 = (f32[256]{0:T(256)S(1)}, f32[256]{0:T(256)}, u32[]{:S(2)}) copy-start(f32[256]{0:T(256)} %get-tuple-element.1086) | copy-start | bytes 3076 | tf_op jit(solution)/shard_map/while
  980.4 15.4 %copy-start.29 = (f32[2048,16]{0,1:T(8,128)S(1)}, f32[2048,16]{0,1:T(8,128)}, u32[]{:S(2)}) copy-start(f32[2048,16]{0,1:T(8,128)} %get-tuple-element.1053) | copy-start | bytes 393220 | tf_op jit(solution)/shard_map/while
  980.4 15.4 %copy-start.31 = (f32[2048,16]{0,1:T(8,128)S(1)}, f32[2048,16]{0,1:T(8,128)}, u32[]{:S(2)}) copy-start(f32[2048,16]{0,1:T(8,128)} %get-tuple-element.1054) | copy-start | bytes 393220 | tf_op jit(solution)/shard_map/while
  981.6 15.7 %copy-start.24 = (f32[256,2048]{1,0:T(8,128)S(1)}, f32[256,2048]{1,0:T(8,128)}, u32[]{:S(2)}) copy-start(f32[256,2048]{1,0:T(8,128)} %copy-done.23) | copy-start | bytes 6291460 | tf_op jit(solution)/shard_map/while
  (47 other events, 113.2 us)
Sparse Core Ops, SparseCore 0:
  1000.8 107.5 all-reduce.2
where the time goes:
time: 1130 us; the launch traced here: 1120 us
  waiting for transfers between devices  362 us (32%)
  other arithmetic  254 us (22%)
  blocking collectives  178 us (16%)
  matrix products  136 us (12%)
  local copies, waits for them, and re-layouts  116 us (10%)
  starting transfers between devices  49.9 us (4%)
  between operations  15 us (1%)
    reduce_sum x8, other arithmetic, grad_block(): jnp.sum(real_rows * d_real.reshape(shape_three) + imag_rows * d_imag.resh...  106 us
    psum x1, waiting for transfers between devices, shards(): lax.psum((res_part, rate_part, gain_part), ('ctx', 'dp'))  104 us
    all_to_all x2, waiting for transfers between devices, spectrum(): lax.all_to_all(slot_imag, 'ctx', split_axis=1, concat_axis=1, tiled=True)  83.3 us
    all_to_all x2, waiting for transfers between devices, positions(): lax.all_to_all(out_real, 'ctx', split_axis=1, concat_axis=1, tiled=True)  75.2 us
    psum x1, blocking collectives, shards(): lax.psum((res_part, rate_part, gain_part), ('ctx', 'dp'))  69.5 us
    reduce_sum x4, other arithmetic, kernel_block(): jnp.sum(f_imag.reshape(block, channels, mode_count) * residue, axis=-1)  60.5 us
    all_to_all x1, blocking collectives, transform_plan(): lax.all_to_all(gate_blk.reshape(batch_rows, ctx_count, slice_len, channel...  52.1 us
    all_to_all x1, blocking collectives, transform_plan(): lax.all_to_all(conv_sl, 'ctx', split_axis=1, concat_axis=1, tiled=True)  51.9 us
  transfers between devices with their start and end apart: 11, of which 8 were waited for; matrix products, arithmetic and copies ran while one was open for 36% of the time, Pallas kernels for 0%

commit v1 on v0

--- a/solution.py
+++ b/solution.py
@@ -96,7 +96,12 @@
         slot_real = jnp.einsum("kb,xbjc->xkjc", forward_real, slices, precision=highest)
         slot_imag = jnp.einsum("kb,xbjc->xkjc", forward_imag, slices, precision=highest)
         rows_real, rows_imag = (
-            lax.all_to_all(slot_real, "ctx", split_axis=1, concat_axis=1, tiled=True),
+            jnp.concatenate(
+                lax.all_to_all(
+                    jnp.stack(jnp.split(slot_real, lax.axis_size("ctx"), axis=1)), "ctx", 0, 0
+                ),
+                axis=1,
+            ),
             lax.all_to_all(slot_imag, "ctx", split_axis=1, concat_axis=1, tiled=True),
         )
         rows_real = rows_real.reshape(batch_rows, length, channels)

time: 1130 us -> 1130 us (level)
  local copies, waits for them, and re-layouts: 116 us -> 133 us
    unnamed x62 -> x76, local copies, waits for them, and re-layouts: 13.1 us -> 33.3 us
where the time goes in v1:
time: 1130 us; the launch traced here: 1120 us
  waiting for transfers between devices  354 us (31%)
  other arithmetic  254 us (22%)
  blocking collectives  179 us (16%)
  local copies, waits for them, and re-layouts  133 us (12%)
  matrix products  127 us (11%)
  starting transfers between devices  50 us (4%)
  between operations  15 us (1%)
    reduce_sum x8, other arithmetic, grad_block(): jnp.sum(real_rows * d_real.reshape(shape_three) + imag_rows * d_imag.resh...  106 us
    psum x1, waiting for transfers between devices, shards(): lax.psum((res_part, rate_part, gain_part), ('ctx', 'dp'))  104 us
    all_to_all x2, waiting for transfers between devices, positions(): lax.all_to_all(out_real, 'ctx', split_axis=1, concat_axis=1, tiled=True)  75.1 us
    all_to_all x2, waiting for transfers between devices, spectrum(): lax.all_to_all(slot_imag, 'ctx', split_axis=1, concat_axis=1, tiled=True)  75.1 us
    psum x1, blocking collectives, shards(): lax.psum((res_part, rate_part, gain_part), ('ctx', 'dp'))  69.4 us
    reduce_sum x4, other arithmetic, kernel_block(): jnp.sum(f_imag.reshape(block, channels, mode_count) * residue, axis=-1)  60.5 us
    all_to_all x1, blocking collectives, transform_plan(): lax.all_to_all(gate_blk.reshape(batch_rows, ctx_count, slice_len, channel...  52.2 us
    all_to_all x1, blocking collectives, transform_plan(): lax.all_to_all(conv_sl, 'ctx', split_axis=1, concat_axis=1, tiled=True)  51.9 us
  transfers between devices with their start and end apart: 11, of which 8 were waited for; matrix products, arithmetic and copies ran while one was open for 36% of the time, Pallas kernels for 0%

profile of v1, /device:TPU:0, one launch (start us, length us, event | category | flops | bytes accessed | tf_op | source)
XLA Modules:
  0.0 1117.4 jit_solution(12563380477410278438)
XLA Ops:
  10.1 7.3 all-to-all-start
  21.5 21.6 %all-to-all-done = bf16[1,8,32,2048]{3,2,0,1:T(8,128)(2,1)S(1)} async-done(((bf16[1,8,32,2048]{3,2,0,1:T(8,128)(2,1)}), bf16[1,8,32,2048]{3,2,0,1:T(8,128)(2,1)S(1)}, u32[]{:S(2)}, u32[]{:S(2)}) %all-to-all-start) | async-done | bytes 1048608 | tf_op jit(solution)/shard_map/all_to_all | solution.py:179
  59.5 39.6 %all-to-all-done.2 = f32[1,8,32,2048]{3,2,0,1:T(8,128)S(1)} async-done(((f32[1,8,32,2048]{3,2,0,1:T(8,128)}), f32[1,8,32,2048]{3,2,0,1:T(8,128)S(1)}, u32[]{:S(2)}, u32[]{:S(2)}) %all-to-all-start.2) | async-done | bytes 2097184 | tf_op jit(solution)/shard_map/all_to_all | solution.py:105
  100.5 4.6 all-to-all-start.1
  105.1 114.4 %while.39 = (s32[]{:T(128)}, f32[4,64,2048]{2,1,0:T(8,128)}, f32[4,64,2048]{2,1,0:T(8,128)}, f32[4,64,2048]{2,1,0:T(8,128)}, f32[4,64,2048]{2,1,0:T(8,128)}, /*i...) while((s32[]{:T(128)}, f32[4,64,2048]{2,1,0:T(8,128)}, ...), condition=%wide.region_5.6_spmd, body=%wide.region_0.5_spmd.sunk | while | flops 70910216 | bytes 10621447 | solution.py:174
  116.4 15.1 %fusion.327 = (f32[64,2048]{1,0:T(8,128)S(1)}, f32[64,2048]{1,0:T(8,128)S(1)}, f32[64,2048]{1,0:T(8,128)S(1)}, f32[64,2048]{1,0:T(8,128)S(1)}) fusion(f32[64]{0:T(128)S(1)} %get-tuple-element.922, f32[64]{0:T(128)S(1)} %get-tuple-element.923, f32[2048,16]{0,1:T(8,128)S(1)} %get-tuple-element.1021, f32[2048,16]{0,1:T(8,128)S(1)} %copy.194, ...), kind=kLoop, calls=%fused_computation.19.clone.1 | loop fusion | flops 70778880 | bytes 2884736 | tf_op jit(solution)/shard_map/while/body/eval_jaxpr/reduce_sum | solution.py:170
  145.0 15.1 %fusion.327 = (f32[64,2048]{1,0:T(8,128)S(1)}, f32[64,2048]{1,0:T(8,128)S(1)}, f32[64,2048]{1,0:T(8,128)S(1)}, f32[64,2048]{1,0:T(8,128)S(1)}) fusion(f32[64]{0:T(128)S(1)} %get-tuple-element.922, f32[64]{0:T(128)S(1)} %get-tuple-element.923, f32[2048,16]{0,1:T(8,128)S(1)} %get-tuple-element.1021, f32[2048,16]{0,1:T(8,128)S(1)} %copy.194, ...), kind=kLoop, calls=%fused_computation.19.clone.1 | loop fusion | flops 70778880 | bytes 2884736 | tf_op jit(solution)/shard_map/while/body/eval_jaxpr/reduce_sum | solution.py:170
  173.6 15.1 %fusion.327 = (f32[64,2048]{1,0:T(8,128)S(1)}, f32[64,2048]{1,0:T(8,128)S(1)}, f32[64,2048]{1,0:T(8,128)S(1)}, f32[64,2048]{1,0:T(8,128)S(1)}) fusion(f32[64]{0:T(128)S(1)} %get-tuple-element.922, f32[64]{0:T(128)S(1)} %get-tuple-element.923, f32[2048,16]{0,1:T(8,128)S(1)} %get-tuple-element.1021, f32[2048,16]{0,1:T(8,128)S(1)} %copy.194, ...), kind=kLoop, calls=%fused_computation.19.clone.1 | loop fusion | flops 70778880 | bytes 2884736 | tf_op jit(solution)/shard_map/while/body/eval_jaxpr/reduce_sum | solution.py:170
  202.2 15.1 %fusion.327 = (f32[64,2048]{1,0:T(8,128)S(1)}, f32[64,2048]{1,0:T(8,128)S(1)}, f32[64,2048]{1,0:T(8,128)S(1)}, f32[64,2048]{1,0:T(8,128)S(1)}) fusion(f32[64]{0:T(128)S(1)} %get-tuple-element.922, f32[64]{0:T(128)S(1)} %get-tuple-element.923, f32[2048,16]{0,1:T(8,128)S(1)} %get-tuple-element.1021, f32[2048,16]{0,1:T(8,128)S(1)} %copy.194, ...), kind=kLoop, calls=%fused_computation.19.clone.1 | loop fusion | flops 70778880 | bytes 2884736 | tf_op jit(solution)/shard_map/while/body/eval_jaxpr/reduce_sum | solution.py:170
  230.6 5.9 convolution_bitcast_fusion.7
  244.2 6.1 multiply_subtract_fusion.2
  250.4 5.8 multiply_add_fusion.6
  259.5 4.8 convolution_subtract_fusion.1
  264.3 6.1 all-to-all-start.3
  270.4 4.9 fusion.51
  275.4 4.7 convolution_add_fusion.3
  280.0 37.6 %all-to-all-done.3 = f32[1,8,32,2048]{3,2,0,1:T(8,128)} async-done(((f32[1,8,32,2048]{3,2,0,1:T(8,128)}), f32[1,8,32,2048]{3,2,0,1:T(8,128)}, u32[]{:S(2)}, u32[]{:S(2)}) %all-to-all-start.3) | async-done | bytes 2097184 | tf_op jit(solution)/shard_map/all_to_all | solution.py:132
  321.8 6.2 fusion.68
  327.9 42.2 %all-to-all-done.4 = f32[1,8,32,2048]{3,2,0,1:T(8,128)S(1)} async-done(((f32[1,8,32,2048]{3,2,0,1:T(8,128)}), f32[1,8,32,2048]{3,2,0,1:T(8,128)S(1)}, u32[]{:S(2)}, u32[]{:S(2)}) %all-to-all-start.4) | async-done | bytes 2097184 | tf_op jit(solution)/shard_map/all_to_all | solution.py:133
  370.1 4.9 fusion.37
  376.2 51.9 %all_to_all.60 = f32[1,8,32,2048]{3,2,0,1:T(8,128)S(1)} all-to-all(f32[1,8,32,2048]{3,2,0,1:T(8,128)S(1)} %copy.126), channel_id=1, replica_groups=mesh['ctx'=8,'chan'=2,'dp'=2] {'ctx'}, dimensions={1} | all-to-all | bytes 4194304 | tf_op jit(solution)/shard_map/all_to_all | solution.py:188
  439.0 52.2 %all_to_all.61 = f32[1,8,32,2048]{3,2,0,1:T(8,128)} all-to-all(f32[1,8,32,2048]{3,2,0,1:T(8,128)S(1)} %bitcast.282), channel_id=1, replica_groups=mesh['ctx'=8,'chan'=2,'dp'=2] {'ctx'}, dimensions={1} | all-to-all | bytes 4194304 | tf_op jit(solution)/shard_map/all_to_all | solution.py:192
  491.2 4.8 convolution_bitcast_fusion.2
  502.2 4.8 convolution_bitcast_fusion.5
  514.5 35.6 %all-to-all-done.8 = f32[1,8,32,2048]{3,2,0,1:T(8,128)S(1)} async-done(((f32[1,8,32,2048]{3,2,0,1:T(8,128)}), f32[1,8,32,2048]{3,2,0,1:T(8,128)S(1)}, u32[]{:S(2)}, u32[]{:S(2)}) %all-to-all-start.8) | async-done | bytes 2097184 | tf_op jit(solution)/shard_map/all_to_all | solution.py:105
  550.1 4.6 all-to-all-start.7
  554.6 5.6 convolution_bitcast_fusion
  560.3 5.7 convolution_bitcast_fusion.1
  566.0 36.3 %all-to-all-done.7 = f32[8,1,1,32,2048]{4,1,3,2,0:T(1,128)} async-done(((f32[8,1,1,32,2048]{4,1,3,2,0:T(1,128)}), f32[8,1,1,32,2048]{4,1,3,2,0:T(1,128)}, u32[]{:S(2)}, u32[]{:S(2)}) %all-to-all-start.7) | async-done | bytes 2097184 | tf_op jit(solution)/shard_map/all_to_all | solution.py:100
  604.7 5.9 convolution_bitcast_fusion.3
  610.6 17.0 %subtract_bitcast_fusion.1 = (f32[256,2048]{0,1:T(8,128)}, f32[256,2048]{0,1:T(8,128)}, f32[256,2048]{0,1:T(8,128)}, f32[256,2048]{0,1:T(8,128)}, f32[1,256,2048...) fusion(f32[1,256,2048]{1,2,0:T(8,128)} %copy-done.7, ...), kind=kOutput, calls=%fused_computation.170 | convolution fusion | flops 1630928896 | bytes 41944064 | tf_op jit(solution)/shard_map/kj,xjc->xkc/dot_general | solution.py:109
  639.9 5.6 fusion.56
  645.4 4.7 convolution_add_fusion.1
  650.1 37.5 %all-to-all-done.9 = f32[1,8,32,2048]{3,2,0,1:T(8,128)} async-done(((f32[1,8,32,2048]{3,2,0,1:T(8,128)}), f32[1,8,32,2048]{3,2,0,1:T(8,128)}, u32[]{:S(2)}, u32[]{:S(2)}) %all-to-all-start.9) | async-done | bytes 2097184 | tf_op jit(solution)/shard_map/all_to_all | solution.py:132
  692.1 69.4 %psum.39 = f32[2048]{0:T(1024)} all-reduce(f32[2048]{0:T(1024)S(1)} %get-tuple-element.596), channel_id=1, replica_groups=mesh['ctx'=8,'chan'=2,'dp'=2] {'ctx','dp'}, use_global_device_ids=true, to_apply=%region_19.20 | all-reduce | flops 2048 | bytes 16384 | tf_op jit(solution)/shard_map/psum | solution.py:268
  771.4 6.2 fusion.60
  777.5 5.5 fusion.36
  785.6 7.2 all-to-all-start.11
  793.4 202.4 %while.40 = (s32[]{:T(128)}, f32[2048,16]{0,1:T(8,128)}, f32[2048,16]{0,1:T(8,128)}, f32[2048,16]{0,1:T(8,128)}, f32[2048,16]{0,1:T(8,128)}, /*index=5*/s32[4]{0...) while((s32[]{:T(128)}, f32[2048,16]{0,1:T(8,128)}, ...), condition=%wide.region_15.16_spmd.clone, body=%wide.region_10.15_spmd.clone.sunk | while | flops 180650240 | bytes 40907724 | solution.py:257
  811.7 13.6 %add_reduce_fusion.8 = (f32[2048,16]{0,1:T(8,128)S(1)}, f32[2048,16]{0,1:T(8,128)S(1)}) fusion(f32[64]{0:T(128)S(1)} %get-tuple-element.965, f32[64,2048]{1,0:T(8,128)S(1)} %copy-done, f32[64]{0:T(128)S(1)} %get-tuple-element.966, f32[64]{0:T(128)S(1)} %get-tuple-element.967, f32[64,2048]{1,0:T(8,128)S(1)} %copy-done.1, f32[2048,16]{0,1:T(8,128)S(1)} %copy.199, ...), kind=kLoop, calls=%fused_computation.71.clone.1 | loop fusion | flops 90112000 | bytes 2360128 | tf_op jit(solution)/shard_map/while/body/eval_jaxpr/reduce_sum | solution.py:248
  829.2 12.9 %add_reduce_fusion.7 = (f32[2048,16]{0,1:T(8,128)S(1)}, f32[2048,16]{0,1:T(8,128)S(1)}) fusion(f32[2048,16]{0,1:T(8,128)S(1)} %copy.199, f32[64]{0:T(128)S(1)} %get-tuple-element.954, f32[2048,16]{0,1:T(8,128)S(1)} %copy.200, f32[2048,16]{0,1:T(8,128)S(1)} %copy.201, f32[64,2048]{1,0:T(8,128)S(1)} %constant_dynamic-slice_fusion.8, ...), kind=kLoop, calls=%fused_computation.75.clone.1 | loop fusion | flops 90112000 | bytes 2360128 | tf_op jit(solution)/shard_map/while/body/eval_jaxpr/reduce_sum | solution.py:248
  861.6 13.6 %add_reduce_fusion.8 = (f32[2048,16]{0,1:T(8,128)S(1)}, f32[2048,16]{0,1:T(8,128)S(1)}) fusion(f32[64]{0:T(128)S(1)} %get-tuple-element.965, f32[64,2048]{1,0:T(8,128)S(1)} %copy-done, f32[64]{0:T(128)S(1)} %get-tuple-element.966, f32[64]{0:T(128)S(1)} %get-tuple-element.967, f32[64,2048]{1,0:T(8,128)S(1)} %copy-done.1, f32[2048,16]{0,1:T(8,128)S(1)} %copy.199, ...), kind=kLoop, calls=%fused_computation.71.clone.1 | loop fusion | flops 90112000 | bytes 2360128 | tf_op jit(solution)/shard_map/while/body/eval_jaxpr/reduce_sum | solution.py:248
  880.0 12.9 %add_reduce_fusion.7 = (f32[2048,16]{0,1:T(8,128)S(1)}, f32[2048,16]{0,1:T(8,128)S(1)}) fusion(f32[2048,16]{0,1:T(8,128)S(1)} %copy.199, f32[64]{0:T(128)S(1)} %get-tuple-element.954, f32[2048,16]{0,1:T(8,128)S(1)} %copy.200, f32[2048,16]{0,1:T(8,128)S(1)} %copy.201, f32[64,2048]{1,0:T(8,128)S(1)} %constant_dynamic-slice_fusion.8, ...), kind=kLoop, calls=%fused_computation.75.clone.1 | loop fusion | flops 90112000 | bytes 2360128 | tf_op jit(solution)/shard_map/while/body/eval_jaxpr/reduce_sum | solution.py:248
  912.4 13.6 %add_reduce_fusion.8 = (f32[2048,16]{0,1:T(8,128)S(1)}, f32[2048,16]{0,1:T(8,128)S(1)}) fusion(f32[64]{0:T(128)S(1)} %get-tuple-element.965, f32[64,2048]{1,0:T(8,128)S(1)} %copy-done, f32[64]{0:T(128)S(1)} %get-tuple-element.966, f32[64]{0:T(128)S(1)} %get-tuple-element.967, f32[64,2048]{1,0:T(8,128)S(1)} %copy-done.1, f32[2048,16]{0,1:T(8,128)S(1)} %copy.199, ...), kind=kLoop, calls=%fused_computation.71.clone.1 | loop fusion | flops 90112000 | bytes 2360128 | tf_op jit(solution)/shard_map/while/body/eval_jaxpr/reduce_sum | solution.py:248
  930.7 12.9 %add_reduce_fusion.7 = (f32[2048,16]{0,1:T(8,128)S(1)}, f32[2048,16]{0,1:T(8,128)S(1)}) fusion(f32[2048,16]{0,1:T(8,128)S(1)} %copy.199, f32[64]{0:T(128)S(1)} %get-tuple-element.954, f32[2048,16]{0,1:T(8,128)S(1)} %copy.200, f32[2048,16]{0,1:T(8,128)S(1)} %copy.201, f32[64,2048]{1,0:T(8,128)S(1)} %constant_dynamic-slice_fusion.8, ...), kind=kLoop, calls=%fused_computation.75.clone.1 | loop fusion | flops 90112000 | bytes 2360128 | tf_op jit(solution)/shard_map/while/body/eval_jaxpr/reduce_sum | solution.py:248
  963.2 13.6 %add_reduce_fusion.8 = (f32[2048,16]{0,1:T(8,128)S(1)}, f32[2048,16]{0,1:T(8,128)S(1)}) fusion(f32[64]{0:T(128)S(1)} %get-tuple-element.965, f32[64,2048]{1,0:T(8,128)S(1)} %copy-done, f32[64]{0:T(128)S(1)} %get-tuple-element.966, f32[64]{0:T(128)S(1)} %get-tuple-element.967, f32[64,2048]{1,0:T(8,128)S(1)} %copy-done.1, f32[2048,16]{0,1:T(8,128)S(1)} %copy.199, ...), kind=kLoop, calls=%fused_computation.71.clone.1 | loop fusion | flops 90112000 | bytes 2360128 | tf_op jit(solution)/shard_map/while/body/eval_jaxpr/reduce_sum | solution.py:248
  981.5 12.9 %add_reduce_fusion.7 = (f32[2048,16]{0,1:T(8,128)S(1)}, f32[2048,16]{0,1:T(8,128)S(1)}) fusion(f32[2048,16]{0,1:T(8,128)S(1)} %copy.199, f32[64]{0:T(128)S(1)} %get-tuple-element.954, f32[2048,16]{0,1:T(8,128)S(1)} %copy.200, f32[2048,16]{0,1:T(8,128)S(1)} %copy.201, f32[64,2048]{1,0:T(8,128)S(1)} %constant_dynamic-slice_fusion.8, ...), kind=kLoop, calls=%fused_computation.75.clone.1 | loop fusion | flops 90112000 | bytes 2360128 | tf_op jit(solution)/shard_map/while/body/eval_jaxpr/reduce_sum | solution.py:248
  1003.4 103.6 %all-reduce.3.cloned.1.call-done = (f32[2048,16]{0,1:T(8,128)}, f32[2048,16]{0,1:T(8,128)}) async-done(((f32[2048,16]{0,1:T(8,128)}, f32[2048,16]{0,1:T(8,128)}), (f32[2048,16]{0,1:T(8,128)}, f32[2048,16]{0,1:T(8,128)})) %all-reduce.3.cloned.1.call-update) | async-done | bytes 262160 | tf_op jit(solution)/shard_map/psum | solution.py:268
  (453 shorter events, 262.9 us)
Async XLA Ops:
  7.2 10.2 copy-start.35
  10.1 33.0 %all-to-all-start = ((bf16[1,8,32,2048]{3,2,0,1:T(8,128)(2,1)}), bf16[1,8,32,2048]{3,2,0,1:T(8,128)(2,1)S(1)}, u32[]{:S(2)}, u32[]{:S(2)}) async-start(bf16[1,8,32,2048]{3,2,0,1:T(8,128)(2,1)} %bitcast.6), calls=%async_computation | async-start | bytes 2097152 | tf_op jit(solution)/shard_map/all_to_all | solution.py:179
  47.1 52.0 %all-to-all-start.2 = ((f32[1,8,32,2048]{3,2,0,1:T(8,128)}), f32[1,8,32,2048]{3,2,0,1:T(8,128)S(1)}, u32[]{:S(2)}, u32[]{:S(2)}) async-start(f32[1,8,32,2048]{3,2,0,1:T(8,128)} %copy.115), calls=%async_computation.2 | async-start | bytes 4194304 | tf_op jit(solution)/shard_map/all_to_all | solution.py:105
  59.5 45.6 %copy-start.26 = (f32[2048,16]{0,1:T(8,128)S(1)}, f32[2048,16]{0,1:T(8,128)}, u32[]{:S(2)}) copy-start(f32[2048,16]{0,1:T(8,128)} %param.16) | copy-start | bytes 393220
  100.5 136.1 %all-to-all-start.1 = ((f32[8,1,1,32,2048]{4,1,3,2,0:T(1,128)}), f32[8,1,1,32,2048]{4,1,3,2,0:T(1,128)}, u32[]{:S(2)}, u32[]{:S(2)}) async-start(f32[8,1,1,32,2048]{4,1,3,2,0:T(1,128)} %fusion.114), calls=%async_computation.1 | async-start | bytes 4194304 | tf_op jit(solution)/shard_map/all_to_all | solution.py:100
  236.5 13.8 %copy-start.6 = (f32[1,256,2048]{1,2,0:T(8,128)}, f32[1,256,2048]{1,2,0:T(8,128)S(1)}, u32[]{:S(2)}) copy-start(f32[1,256,2048]{1,2,0:T(8,128)S(1)} %convolution_bitcast_fusion.7) | copy-start | bytes 6291460
  236.6 7.6 copy-start.20
  244.2 6.1 copy-start.7
  244.2 6.1 copy-start.10
  244.2 6.1 copy-start.11
  250.3 5.9 copy-start.12
  250.4 9.1 copy-start.14
  264.3 6.1 copy-start.15
  264.3 53.4 %all-to-all-start.3 = ((f32[1,8,32,2048]{3,2,0,1:T(8,128)}), f32[1,8,32,2048]{3,2,0,1:T(8,128)}, u32[]{:S(2)}, u32[]{:S(2)}) async-start(f32[1,8,32,2048]{3,2,0,1:T(8,128)} %bitcast.281), calls=%async_computation.3 | async-start | bytes 4194304 | tf_op jit(solution)/shard_map/all_to_all | solution.py:132
  317.7 52.4 %all-to-all-start.4 = ((f32[1,8,32,2048]{3,2,0,1:T(8,128)}), f32[1,8,32,2048]{3,2,0,1:T(8,128)S(1)}, u32[]{:S(2)}, u32[]{:S(2)}) async-start(f32[1,8,32,2048]{3,2,0,1:T(8,128)} %bitcast.52), calls=%async_computation.4 | async-start | bytes 4194304 | tf_op jit(solution)/shard_map/all_to_all | solution.py:133
  376.2 52.0 %copy-start.24 = (bf16[1,256,2048]{2,1,0:T(8,128)(2,1)S(1)}, bf16[1,256,2048]{2,1,0:T(8,128)(2,1)}, u32[]{:S(2)}) copy-start(bf16[1,256,2048]{2,1,0:T(8,128)(2,1)} %param.11) | copy-start | bytes 3145732
  498.5 51.5 %all-to-all-start.8 = ((f32[1,8,32,2048]{3,2,0,1:T(8,128)}), f32[1,8,32,2048]{3,2,0,1:T(8,128)S(1)}, u32[]{:S(2)}, u32[]{:S(2)}) async-start(f32[1,8,32,2048]{3,2,0,1:T(8,128)} %copy.131), calls=%async_computation.8 | async-start | bytes 4194304 | tf_op jit(solution)/shard_map/all_to_all | solution.py:105
  550.1 52.2 %all-to-all-start.7 = ((f32[8,1,1,32,2048]{4,1,3,2,0:T(1,128)}), f32[8,1,1,32,2048]{4,1,3,2,0:T(1,128)}, u32[]{:S(2)}, u32[]{:S(2)}) async-start(f32[8,1,1,32,2048]{4,1,3,2,0:T(1,128)} %fusion.106), calls=%async_computation.7 | async-start | bytes 4194304 | tf_op jit(solution)/shard_map/all_to_all | solution.py:100
  627.6 7.7 copy-start.4
  627.6 7.7 copy-start.5
  635.3 52.3 %all-to-all-start.9 = ((f32[1,8,32,2048]{3,2,0,1:T(8,128)}), f32[1,8,32,2048]{3,2,0,1:T(8,128)}, u32[]{:S(2)}, u32[]{:S(2)}) async-start(f32[1,8,32,2048]{3,2,0,1:T(8,128)} %bitcast.280), calls=%async_computation.9 | async-start | bytes 4194304 | tf_op jit(solution)/shard_map/all_to_all | solution.py:132
  687.7 89.9 %all-to-all-start.10 = ((f32[1,8,32,2048]{3,2,0,1:T(8,128)}), f32[1,8,32,2048]{3,2,0,1:T(8,128)}, u32[]{:S(2)}, u32[]{:S(2)}) async-start(f32[1,8,32,2048]{3,2,0,1:T(8,128)} %bitcast.279), calls=%async_computation.10 | async-start | bytes 4194304 | tf_op jit(solution)/shard_map/all_to_all | solution.py:133
  785.6 213.7 %all-to-all-start.11 = ((f32[1,8,32,2048]{3,2,0,1:T(8,128)}), f32[1,8,32,2048]{3,2,0,1:T(8,128)}, u32[]{:S(2)}, u32[]{:S(2)}) async-start(f32[1,8,32,2048]{3,2,0,1:T(8,128)} %copy.142), calls=%async_computation.11 | async-start | bytes 4194304 | tf_op jit(solution)/shard_map/all_to_all | solution.py:201
  792.8 314.2 %all-reduce.3.cloned.1.call-start = ((), (), s32[]{:S(2)}) async-start(), calls=%async_computation.12 | async-start | bytes 524288 | tf_op jit(solution)/shard_map/psum | solution.py:268
  793.6 6.0 copy-start.22
  811.1 14.3 %copy-start.32 = (f32[2048,16]{0,1:T(8,128)S(1)}, f32[2048,16]{0,1:T(8,128)}, u32[]{:S(2)}) copy-start(f32[2048,16]{0,1:T(8,128)} %get-tuple-element.1055) | copy-start | bytes 393220 | tf_op jit(solution)/shard_map/while
  811.7 14.4 %copy-start.37 = (f32[256]{0:T(256)S(1)}, f32[256]{0:T(256)}, u32[]{:S(2)}) copy-start(f32[256]{0:T(256)} %get-tuple-element.1086) | copy-start | bytes 3076 | tf_op jit(solution)/shard_map/while
  826.7 15.4 %copy-start.28 = (f32[2048,16]{0,1:T(8,128)S(1)}, f32[2048,16]{0,1:T(8,128)}, u32[]{:S(2)}) copy-start(f32[2048,16]{0,1:T(8,128)} %get-tuple-element.1053) | copy-start | bytes 393220 | tf_op jit(solution)/shard_map/while
  826.7 15.4 %copy-start.30 = (f32[2048,16]{0,1:T(8,128)S(1)}, f32[2048,16]{0,1:T(8,128)}, u32[]{:S(2)}) copy-start(f32[2048,16]{0,1:T(8,128)} %get-tuple-element.1054) | copy-start | bytes 393220 | tf_op jit(solution)/shard_map/while
  827.8 15.6 %copy-start.23 = (f32[256,2048]{1,0:T(8,128)S(1)}, f32[256,2048]{1,0:T(8,128)}, u32[]{:S(2)}) copy-start(f32[256,2048]{1,0:T(8,128)} %copy-done.22) | copy-start | bytes 6291460 | tf_op jit(solution)/shard_map/while
  843.5 6.0 copy-start.22
  860.9 14.3 %copy-start.32 = (f32[2048,16]{0,1:T(8,128)S(1)}, f32[2048,16]{0,1:T(8,128)}, u32[]{:S(2)}) copy-start(f32[2048,16]{0,1:T(8,128)} %get-tuple-element.1055) | copy-start | bytes 393220 | tf_op jit(solution)/shard_map/while
  861.6 15.3 %copy-start.37 = (f32[256]{0:T(256)S(1)}, f32[256]{0:T(256)}, u32[]{:S(2)}) copy-start(f32[256]{0:T(256)} %get-tuple-element.1086) | copy-start | bytes 3076 | tf_op jit(solution)/shard_map/while
  877.5 15.4 %copy-start.28 = (f32[2048,16]{0,1:T(8,128)S(1)}, f32[2048,16]{0,1:T(8,128)}, u32[]{:S(2)}) copy-start(f32[2048,16]{0,1:T(8,128)} %get-tuple-element.1053) | copy-start | bytes 393220 | tf_op jit(solution)/shard_map/while
  877.5 15.4 %copy-start.30 = (f32[2048,16]{0,1:T(8,128)S(1)}, f32[2048,16]{0,1:T(8,128)}, u32[]{:S(2)}) copy-start(f32[2048,16]{0,1:T(8,128)} %get-tuple-element.1054) | copy-start | bytes 393220 | tf_op jit(solution)/shard_map/while
  878.6 15.6 %copy-start.23 = (f32[256,2048]{1,0:T(8,128)S(1)}, f32[256,2048]{1,0:T(8,128)}, u32[]{:S(2)}) copy-start(f32[256,2048]{1,0:T(8,128)} %copy-done.22) | copy-start | bytes 6291460 | tf_op jit(solution)/shard_map/while
  894.3 6.0 copy-start.22
  911.7 14.3 %copy-start.32 = (f32[2048,16]{0,1:T(8,128)S(1)}, f32[2048,16]{0,1:T(8,128)}, u32[]{:S(2)}) copy-start(f32[2048,16]{0,1:T(8,128)} %get-tuple-element.1055) | copy-start | bytes 393220 | tf_op jit(solution)/shard_map/while
  912.4 15.3 %copy-start.37 = (f32[256]{0:T(256)S(1)}, f32[256]{0:T(256)}, u32[]{:S(2)}) copy-start(f32[256]{0:T(256)} %get-tuple-element.1086) | copy-start | bytes 3076 | tf_op jit(solution)/shard_map/while
  928.3 15.4 %copy-start.28 = (f32[2048,16]{0,1:T(8,128)S(1)}, f32[2048,16]{0,1:T(8,128)}, u32[]{:S(2)}) copy-start(f32[2048,16]{0,1:T(8,128)} %get-tuple-element.1053) | copy-start | bytes 393220 | tf_op jit(solution)/shard_map/while
  928.3 15.4 %copy-start.30 = (f32[2048,16]{0,1:T(8,128)S(1)}, f32[2048,16]{0,1:T(8,128)}, u32[]{:S(2)}) copy-start(f32[2048,16]{0,1:T(8,128)} %get-tuple-element.1054) | copy-start | bytes 393220 | tf_op jit(solution)/shard_map/while
  929.4 15.6 %copy-start.23 = (f32[256,2048]{1,0:T(8,128)S(1)}, f32[256,2048]{1,0:T(8,128)}, u32[]{:S(2)}) copy-start(f32[256,2048]{1,0:T(8,128)} %copy-done.22) | copy-start | bytes 6291460 | tf_op jit(solution)/shard_map/while
  945.0 6.0 copy-start.22
  962.5 14.3 %copy-start.32 = (f32[2048,16]{0,1:T(8,128)S(1)}, f32[2048,16]{0,1:T(8,128)}, u32[]{:S(2)}) copy-start(f32[2048,16]{0,1:T(8,128)} %get-tuple-element.1055) | copy-start | bytes 393220 | tf_op jit(solution)/shard_map/while
  963.1 15.3 %copy-start.37 = (f32[256]{0:T(256)S(1)}, f32[256]{0:T(256)}, u32[]{:S(2)}) copy-start(f32[256]{0:T(256)} %get-tuple-element.1086) | copy-start | bytes 3076 | tf_op jit(solution)/shard_map/while
  979.0 15.4 %copy-start.28 = (f32[2048,16]{0,1:T(8,128)S(1)}, f32[2048,16]{0,1:T(8,128)}, u32[]{:S(2)}) copy-start(f32[2048,16]{0,1:T(8,128)} %get-tuple-element.1053) | copy-start | bytes 393220 | tf_op jit(solution)/shard_map/while
  979.1 15.4 %copy-start.30 = (f32[2048,16]{0,1:T(8,128)S(1)}, f32[2048,16]{0,1:T(8,128)}, u32[]{:S(2)}) copy-start(f32[2048,16]{0,1:T(8,128)} %get-tuple-element.1054) | copy-start | bytes 393220 | tf_op jit(solution)/shard_map/while
  980.2 15.6 %copy-start.23 = (f32[256,2048]{1,0:T(8,128)S(1)}, f32[256,2048]{1,0:T(8,128)}, u32[]{:S(2)}) copy-start(f32[256,2048]{1,0:T(8,128)} %copy-done.22) | copy-start | bytes 6291460 | tf_op jit(solution)/shard_map/while
  (46 other events, 100.5 us)
Sparse Core Ops, SparseCore 0:
  999.4 107.5 all-reduce.2
